TPU v7x, 32 devices: a whole 2x2x4 slice. The times are simulated.
32 devices in a mesh: dp: 8 (over z, y), shard: 4 (over x, core).
Axes of the slice: x: 2, y: 2, z: 4, core: 2. Of those that a mesh axis runs over, the one named last changes fastest.
Arguments:
- tokens: bfloat16 [13312, 4096], P(('dp', 'shard')), may hold values from -6 to 6
- cotangent: bfloat16 [13312, 4096], P(('dp', 'shard')), may hold values from -6 to 6
- gate_up: bfloat16 [4, 4096, 256], P('shard'), may hold values from -0.09375 to 0.09375
- down: bfloat16 [4, 128, 4096], P('shard'), may hold values from -0.09375 to 0.09375
- kept_slots: int32 [2], replicated, may hold values from 0 to 3, as said below
Outputs:
- token_grad: bfloat16 [13312, 4096], P(('dp', 'shard'))
- grad_gate_up: bfloat16 [4, 4096, 256], P('shard', 'dp')
- grad_down: bfloat16 [4, 128, 4096], P('shard', None, 'dp')
Inputs may be any that keep to these rules, and one draw needn't show every extreme that they name: `kept_slots`: 2 distinct positions; position p is stored on index p // 1 of shard.
All inputs are finite; a program needn't handle non-finite values.
Results may differ from a plain program's by a relative error of at most 0.015.
Values may be sent and summed in bfloat16 or wider, within the bound.
A program may use at most 128 MiB of HBM per device.

v0:
```python
import math
import jax
import jax.numpy as jnp
from jax import lax
from jax.sharding import PartitionSpec as P


def spread(block, axis, source):
    block = jnp.where(lax.axis_index(axis) == source, block, jnp.zeros_like(block))
    return lax.psum(block, axis)


def body(tokens, cotangent, gate_up, down, kept_slots):
    slot_count = gate_up.shape[0]
    block_cols = down.shape[1]
    kept_count = kept_slots.shape[0]
    total_tokens = tokens.shape[0] * lax.axis_size("dp") * lax.axis_size("shard")
    scale_factor = 1.0 / math.sqrt(total_tokens)
    dx_total = jnp.zeros(tokens.shape, jnp.float32)
    pair_terms = []
    back_terms = []
    for kept_pos in range(kept_count):
        slot_id = kept_slots[kept_pos]
        local_slot = slot_id % slot_count
        owner_id = slot_id // slot_count
        own_pair = lax.dynamic_index_in_dim(gate_up, local_slot, 0, keepdims=False)
        own_back = lax.dynamic_index_in_dim(down, local_slot, 0, keepdims=False)
        w_pair, w_back = (spread(own_pair, "shard", owner_id), spread(own_back, "shard", owner_id))
        projected = jnp.dot(tokens, w_pair, preferred_element_type=jnp.float32)
        gate_pre = projected[:, :block_cols]
        up_pre = projected[:, block_cols:]
        sigmoid_gate = jax.nn.sigmoid(gate_pre)
        silu_gate = gate_pre * sigmoid_gate
        activated = (silu_gate * up_pre).astype(jnp.bfloat16)
        d_act = lax.dot_general(
            cotangent, w_back, (((1,), (1,)), ((), ())), preferred_element_type=jnp.float32
        )
        d_gate = d_act * up_pre * sigmoid_gate * (1.0 + gate_pre * (1.0 - sigmoid_gate))
        d_up = d_act * silu_gate
        d_projected = jnp.concatenate([d_gate, d_up], axis=1).astype(jnp.bfloat16)
        dx_total = dx_total + lax.dot_general(
            d_projected, w_pair, (((1,), (1,)), ((), ())), preferred_element_type=jnp.float32
        )
        pair_terms.append(
            lax.dot_general(
                tokens, d_projected, (((0,), (0,)), ((), ())), preferred_element_type=jnp.float32
            )
        )
        back_terms.append(
            lax.dot_general(
                activated, cotangent, (((0,), (0,)), ((), ())), preferred_element_type=jnp.float32
            )
        )
    pair_stack = jnp.stack(pair_terms)
    back_stack = jnp.stack(back_terms)
    pair_part, back_part = (
        lax.psum_scatter(
            pair_stack.astype(jnp.bfloat16), "dp", scatter_dimension=1, tiled=True
        ).astype(jnp.float32),
        lax.psum_scatter(
            back_stack.astype(jnp.bfloat16), "dp", scatter_dimension=2, tiled=True
        ).astype(jnp.float32),
    )
    pair_whole, back_whole = (
        lax.psum(pair_part.astype(jnp.bfloat16), "shard").astype(jnp.float32),
        lax.psum(back_part.astype(jnp.bfloat16), "shard").astype(jnp.float32),
    )
    my_slots = lax.axis_index("shard") * slot_count + jnp.arange(slot_count, dtype=jnp.int32)
    picking = (my_slots[:, None] == kept_slots[None, :]).astype(jnp.float32)
    pair_owned = jnp.einsum("sk,kab->sab", picking, pair_whole, precision=lax.Precision.HIGHEST)
    back_owned = jnp.einsum("sk,kab->sab", picking, back_whole, precision=lax.Precision.HIGHEST)
    return (
        dx_total.astype(jnp.bfloat16),
        (pair_owned * scale_factor).astype(jnp.bfloat16),
        (back_owned * scale_factor).astype(jnp.bfloat16),
    )


def solution(mesh):
    in_specs = (
        P(("dp", "shard"), None),
        P(("dp", "shard"), None),
        P("shard", None, None),
        P("shard", None, None),
        P(),
    )
    out_specs = (P(("dp", "shard"), None), P("shard", "dp", None), P("shard", None, "dp"))
    return jax.shard_map(body, mesh=mesh, in_specs=in_specs, out_specs=out_specs, check_vma=False)
```

profile of v0, /device:TPU:0, one launch (start us, length us, event | category | flops | bytes accessed | tf_op | source)
XLA Modules:
  0.0 355.7 jit_solution(2671473297520610019)
XLA Ops:
  7.2 0.0 copy-start
  7.2 0.0 all-reduce.7.cloned.1.call-start
  7.2 1.4 fusion.21
  9.9 0.0 copy-start.4
  10.0 2.9 select_bitcast_fusion.2
  12.8 0.0 copy-done.4
  12.8 2.3 select_bitcast_fusion
  15.1 0.0 all-reduce.7.cloned.1.call-update
  15.1 0.0 reduce-scatter.5.cloned.1.call-start
  15.2 122.9 %all-reduce.7.cloned.1.call-done = (bf16[4096,256]{1,0:T(8,128)(2,1)}, bf16[128,4096]{1,0:T(8,128)(2,1)}, bf16[4096,256]{1,0:T(8,128)(2,1)}, bf16[128,4096]{1,0:T(8,128)(2,1)}) async-done(((bf16[4096,256]{1,0:T(8,128)(2,1)}, bf16[128,4096]{1,0:T(8,128)(2,1)}, bf16[4096,256]{1,0:T(8,128)(2,1)}, bf16[128,4096]{1,0:T(8,128)(2,1)}), (bf16[4096,256]{1,0:T(8,128)(2,1)}, bf16[128,4096]{1,0:T(8,128)(2,1)}, ...) | async-done | bytes 6291472 | tf_op jit(solution)/shard_map/psum | solution.py:10
  138.1 0.0 copy-done
  138.1 0.0 copy-start.3
  138.1 2.8 convolution_bitcast_fusion.1
  140.9 0.0 copy-start.8
  140.9 0.0 copy-done.3
  140.9 0.0 copy-start.1
  141.0 1.1 convolution_bitcast_fusion
  142.0 1.0 copy-done.1
  143.1 0.0 copy-start.10
  143.1 0.8 fusion.3
  143.8 0.0 copy-done.8
  143.9 0.8 fusion.2
  144.6 0.0 copy-done.10
  144.6 1.5 pad_maximum_fusion.1
  146.2 0.0 reduce-scatter.5.cloned.1.call-update
  146.2 0.0 reduce-scatter.3.cloned.1.call-start
  146.2 3.4 multiply_convert_fusion.3
  149.6 0.0 copy-start.5
  149.6 0.0 copy-start.2
  149.6 0.0 copy-start.9
  149.7 0.0 copy-start.12
  149.7 1.3 fusion.1
  150.9 0.0 copy-done.5
  151.0 0.7 copy-done.2
  151.6 0.1 copy-done.9
  151.7 0.3 copy-done.12
  152.0 1.1 multiply_convert_fusion.5
  153.1 0.0 copy-start.6
  153.1 0.0 copy-start.7
  153.1 0.6 copy-done.6
  153.8 0.0 copy-done.7
  153.8 1.3 fusion
  155.1 2.4 pad_maximum_fusion
  157.5 0.0 copy-start.11
  157.5 0.0 reduce-scatter.3.cloned.1.call-update
  157.5 0.2 all-reduce.5.cloned.1.call-start
  157.8 0.4 copy-done.11
  158.2 5.7 %fusion.11 = f32[416,4096]{1,0:T(8,128)} fusion(bf16[4096,256]{1,0:T(8,128)(2,1)} %get-tuple-element.5, bf16[416,128]{1,0:T(8,128)(2,1)} %copy-done.7, bf16[416,128]{1,0:T(8,128)(2,1)} %copy-done.6), kind=kOutput, calls=%fused_computation.38 | convolution fusion | flops 872841216 | bytes 9125888 | tf_op jit(solution)/shard_map/dot_general | solution.py:41
  163.8 50.8 %reduce-scatter.5.cloned.1.call-done = bf16[2,128,512]{2,1,0:T(8,128)(2,1)} async-done(((bf16[2,128,4096]{2,1,0:T(8,128)(2,1)}), bf16[2,128,512]{2,1,0:T(8,128)(2,1)}) %reduce-scatter.5.cloned.1.call-update) | async-done | bytes 262160 | tf_op jit(solution)/shard_map/reduce_scatter | solution.py:60
  214.7 91.0 %reduce-scatter.3.cloned.1.call-done = bf16[2,512,256]{1,2,0:T(8,128)(2,1)} async-done(((bf16[2,4096,256]{1,2,0:T(8,128)(2,1)}), bf16[2,512,256]{1,2,0:T(8,128)(2,1)}) %reduce-scatter.3.cloned.1.call-update) | async-done | bytes 524304 | tf_op jit(solution)/shard_map/reduce_scatter | solution.py:57
  305.6 0.0 all-reduce.5.cloned.1.call-update
  305.7 6.4 %add_convert_fusion = bf16[416,4096]{1,0:T(8,128)(2,1)} fusion(f32[416,4096]{1,0:T(8,128)} %fusion.11, bf16[4096,256]{1,0:T(8,128)(2,1)} %get-tuple-element.7, bf16[416,128]{1,0:T(8,128)(2,1)} %copy-done.5, bf16[416,128]{1,0:T(8,128)(2,1)S(1)} %get-tuple-element.13), kind=kOutput, calls=%fused_computation | convolution fusion | flops 876249088 | bytes 12533760 | tf_op jit(solution)/shard_map/dot_general | solution.py:41
  312.1 30.5 %all-reduce.5.cloned.1.call-done = (bf16[2,512,256]{1,2,0:T(8,128)(2,1)}, bf16[2,128,512]{2,1,0:T(8,128)(2,1)}) async-done(((bf16[2,512,256]{1,2,0:T(8,128)(2,1)}, bf16[2,128,512]{2,1,0:T(8,128)(2,1)}), (bf16[2,512,256]{1,2,0:T(8,128)(2,1)}, bf16[2,128,512]{2,1,0:T(8,128)(2,1)})) %all-reduce.5.cloned.1.call-update) | async-done | bytes 786448 | tf_op jit(solution)/shard_map/psum | solution.py:65
  342.6 2.0 copy.8
  344.6 1.7 fusion.22
  346.3 0.8 fusion.5
  347.1 1.4 fusion.7
  348.4 0.7 fusion.12
  (1 shorter events, 0.0 us)
Async XLA Ops:
  7.2 131.0 %copy-start = (bf16[416,4096]{1,0:T(8,128)(2,1)S(1)}, bf16[416,4096]{1,0:T(8,128)(2,1)}, u32[]{:S(2)}) copy-start(bf16[416,4096]{1,0:T(8,128)(2,1)} %param.5) | copy-start | bytes 10223620
  7.2 130.9 %all-reduce.7.cloned.1.call-start = ((), (), s32[]{:S(2)}) async-start(), calls=%async_computation.5 | async-start | bytes 12582912 | tf_op jit(solution)/shard_map/psum | solution.py:10
  9.9 2.9 copy-start.4
  15.1 199.5 %reduce-scatter.5.cloned.1.call-start = ((), (), s32[]{:S(2)}) async-start(), calls=%async_computation.3 | async-start | bytes 2359296 | tf_op jit(solution)/shard_map/reduce_scatter | solution.py:60
  138.1 2.8 copy-start.3
  140.9 2.9 copy-start.8
  140.9 2.1 copy-start.1
  143.1 1.6 copy-start.10
  146.2 159.5 %reduce-scatter.3.cloned.1.call-start = ((), (), s32[]{:S(2)}) async-start(), calls=%async_computation.2 | async-start | bytes 4718592 | tf_op jit(solution)/shard_map/reduce_scatter | solution.py:57
  149.6 1.3 copy-start.5
  149.6 2.0 copy-start.2
  149.6 2.1 copy-start.9
  149.7 2.4 copy-start.12
  153.1 0.6 copy-start.6
  153.1 0.7 copy-start.7
  157.5 0.7 copy-start.11
  157.5 185.1 %all-reduce.5.cloned.1.call-start = ((), (), s32[]{:S(2)}) async-start(), calls=%async_computation.4 | async-start | bytes 1572864 | tf_op jit(solution)/shard_map/psum | solution.py:65
Sparse Core Ops, SparseCore 0:
  15.2 122.8 all-reduce.6
  146.3 68.3 reduce-scatter.4
  218.3 87.3 reduce-scatter.2
  308.1 34.3 all-reduce.4
where the time goes:
time: 356 us
  waiting for transfers between devices  295 us (83%)
  matrix products  27.6 us (8%)
  between operations  15.2 us (4%)
  other arithmetic  10.5 us (3%)
  local copies, waits for them, and re-layouts  6.64 us (2%)
    psum x1, waiting for transfers between devices, spread(): return lax.psum(block, axis)  123 us
    reduce_scatter x1, waiting for transfers between devices, body(): lax.psum_scatter(pair_stack.astype(jnp.bfloat16), 'dp', scatter_dimension...  91 us
    reduce_scatter x1, waiting for transfers between devices, body(): lax.psum_scatter(back_stack.astype(jnp.bfloat16), 'dp', scatter_dimension...  50.8 us
    psum x1, waiting for transfers between devices, body(): lax.psum(pair_part.astype(jnp.bfloat16), 'shard').astype(jnp.float32)  30.5 us
    dot_general x2, matrix products, body(): lax.dot_general(d_projected, w_pair, (((1,), (1,)), ((), ())), preferred_...  12.1 us
  transfers between devices with their start and end apart: 4, of which 4 were waited for; matrix products, arithmetic and copies ran while one was open for 6% of the time, Pallas kernels for 0%

commit v1 on v0

--- a/solution.py
+++ b/solution.py
@@ -62,7 +62,9 @@
         ).astype(jnp.float32),
     )
     pair_whole, back_whole = (
-        lax.psum(pair_part.astype(jnp.bfloat16), "shard").astype(jnp.float32),
+        jnp.sum(lax.all_gather(pair_part.astype(jnp.bfloat16), "shard"), axis=0).astype(
+            jnp.float32
+        ),
         lax.psum(back_part.astype(jnp.bfloat16), "shard").astype(jnp.float32),
     )
     my_slots = lax.axis_index("shard") * slot_count + jnp.arange(slot_count, dtype=jnp.int32)

time: 356 us -> 372 us (1.045)
  waiting for transfers between devices: 295 us -> 315 us
  matrix products: 27.6 us -> 21.4 us
  other arithmetic: 10.5 us -> 14.6 us
    psum x1 -> x0, waiting for transfers between devices: 30.5 us -> none  [body(): lax.psum(pair_part.astype(jnp.bfloat16), 'shard').astype(jnp.float32)]
    psum x1 -> x2, waiting for transfers between devices: 123 us -> 146 us  [spread(): return lax.psum(block, axis)]
    reduce_scatter x1, waiting for transfers between devices: 50.8 us -> 65.8 us  [body(): lax.psum_scatter(back_stack.astype(jnp.bfloat16), 'dp', scatter_dimension...]
    all_gather x0 -> x1, waiting for transfers between devices: none -> 14.6 us  [body(): lax.all_gather(pair_part.astype(jnp.bfloat16), 'shard')]
    dot_general x2, matrix products: 12.1 us -> 5.79 us  [body(): lax.dot_general(d_projected, w_pair, (((1,), (1,)), ((), ())), preferred_...]
  transfers between devices with their start and end apart: 4 -> 5, of which waited for: 4 -> 5; matrix products, arithmetic and copies ran while one was open for 6% -> 3% of each run, Pallas kernels for 0% -> 0%
where the time goes in v1:
time: 372 us
  waiting for transfers between devices  315 us (85%)
  matrix products  21.4 us (6%)
  between operations  15.3 us (4%)
  other arithmetic  14.6 us (4%)
  local copies, waits for them, and re-layouts  4.79 us (1%)
    psum x2, waiting for transfers between devices, spread(): return lax.psum(block, axis)  146 us
    reduce_scatter x1, waiting for transfers between devices, body(): lax.psum_scatter(pair_stack.astype(jnp.bfloat16), 'dp', scatter_dimension...  88.2 us
    reduce_scatter x1, waiting for transfers between devices, body(): lax.psum_scatter(back_stack.astype(jnp.bfloat16), 'dp', scatter_dimension...  65.8 us
    all_gather x1, waiting for transfers between devices, body(): lax.all_gather(pair_part.astype(jnp.bfloat16), 'shard')  14.6 us
  transfers between devices with their start and end apart: 5, of which 5 were waited for; matrix products, arithmetic and copies ran while one was open for 3% of the time, Pallas kernels for 0%

profile of v1, /device:TPU:0, one launch (start us, length us, event | category | flops | bytes accessed | tf_op | source)
XLA Modules:
  0.0 371.6 jit_solution(14715146809960354296)
XLA Ops:
  7.2 0.0 copy-start
  7.2 0.0 all-reduce.7.cloned.1.call-start
  7.2 1.4 fusion.23
  9.9 3.9 %select_bitcast_fusion = (bf16[4096,256]{1,0:T(8,128)(2,1)}, bf16[4096,256]{1,0:T(8,128)(2,1)}) fusion(bf16[1,4096,256]{2,1,0:T(8,128)(2,1)} %param.7, pred[]{:T(512)S(6)} %eq.21, pred[]{:T(512)S(6)} %eq.20), kind=kLoop, calls=%fused_computation.11 | loop fusion | flops 2097152 | bytes 6291458 | tf_op jit(solution)/shard_map/jit(_where)/select_n | solution.py:9
  13.8 0.0 all-reduce.7.cloned.1.call-update
  13.8 0.0 reduce-scatter.5.cloned.1.call-start
  13.9 88.5 %all-reduce.7.cloned.1.call-done = (bf16[4096,256]{1,0:T(8,128)(2,1)}, bf16[4096,256]{1,0:T(8,128)(2,1)}) async-done(((bf16[4096,256]{1,0:T(8,128)(2,1)}, bf16[4096,256]{1,0:T(8,128)(2,1)}), (bf16[4096,256]{1,0:T(8,128)(2,1)}, bf16[4096,256]{1,0:T(8,128)(2,1)})) %all-reduce.7.cloned.1.call-update) | async-done | bytes 4194320 | tf_op jit(solution)/shard_map/psum | solution.py:10
  102.4 0.0 copy-done
  102.4 0.0 copy-start.3
  102.4 2.8 convolution_bitcast_fusion.1
  105.2 0.0 copy-start.11
  105.2 0.0 copy-done.3
  105.2 0.0 copy-start.1
  105.2 1.1 convolution_bitcast_fusion
  106.3 1.0 copy-done.1
  107.3 0.0 copy-start.9
  107.3 0.8 fusion.3
  108.1 0.0 copy-done.11
  108.1 0.8 fusion.2
  108.9 0.0 copy-done.9
  108.9 1.5 pad_maximum_fusion.1
  110.4 0.0 reduce-scatter.5.cloned.1.call-update
  110.4 0.0 all-reduce.5.cloned.1.call-start
  110.5 2.7 select_bitcast_fusion.2
  113.1 65.8 %reduce-scatter.5.cloned.1.call-done = bf16[2,128,512]{2,1,0:T(8,128)(2,1)} async-done(((bf16[2,128,4096]{2,1,0:T(8,128)(2,1)}), bf16[2,128,512]{2,1,0:T(8,128)(2,1)}) %reduce-scatter.5.cloned.1.call-update) | async-done | bytes 262160 | tf_op jit(solution)/shard_map/reduce_scatter | solution.py:60
  179.0 0.0 all-reduce.5.cloned.1.call-update
  179.0 0.0 reduce-scatter.3.cloned.1.call-start
  179.0 57.8 %all-reduce.5.cloned.1.call-done = (bf16[128,4096]{1,0:T(8,128)(2,1)}, bf16[128,4096]{1,0:T(8,128)(2,1)}, bf16[2,128,512]{2,1,0:T(8,128)(2,1)}) async-done(((bf16[128,4096]{1,0:T(8,128)(2,1)}, bf16[128,4096]{1,0:T(8,128)(2,1)}, bf16[2,128,512]{2,1,0:T(8,128)(2,1)}), (bf16[128,4096]{1,0:T(8,128)(2,1)}, bf16[128,4096]{1,0:T(8,128)(2,1)}, bf16[2,128,512]{2,1,0:T(8,128)(2,1)})) %all-reduce.5.cloned.1.call-update) | async-done | bytes 2359312 | tf_op jit(solution)/shard_map/psum | solution.py:10
  236.8 0.0 copy-start.2
  236.8 0.0 copy-start.10
  236.8 0.0 copy-start.13
  236.8 3.5 multiply_convert_fusion.5
  240.4 0.0 copy-start.7
  240.4 0.0 copy-start.8
  240.4 0.0 copy-done.2
  240.4 0.0 copy-done.10
  240.4 0.2 copy-done.13
  240.7 1.1 multiply_convert_fusion.3
  241.7 0.0 copy-start.5
  241.8 1.3 fusion.1
  243.0 0.0 copy-done.5
  243.0 0.0 copy-done.7
  243.1 0.0 copy-done.8
  243.1 1.3 fusion
  244.3 2.3 pad_maximum_fusion
  246.6 0.0 copy-start.12
  246.6 0.0 reduce-scatter.3.cloned.1.call-update
  246.7 0.2 all-gather.3.cloned.1.call-start
  246.9 88.2 %reduce-scatter.3.cloned.1.call-done = bf16[2,512,256]{1,2,0:T(8,128)(2,1)} async-done(((bf16[2,4096,256]{1,2,0:T(8,128)(2,1)}), bf16[2,512,256]{1,2,0:T(8,128)(2,1)}) %reduce-scatter.3.cloned.1.call-update) | async-done | bytes 524304 | tf_op jit(solution)/shard_map/reduce_scatter | solution.py:57
  335.2 2.0 copy.8
  337.2 0.0 all-gather.3.cloned.1.call-update
  337.2 0.0 copy-done.12
  337.2 1.4 fusion.9
  338.6 0.7 fusion.14
  339.3 0.0 copy-start.4
  339.3 0.0 copy-start.6
  339.3 2.9 fusion.13
  342.2 0.0 copy-done.4
  342.2 0.0 copy-done.6
  342.2 2.9 add_convert_fusion
  345.1 14.6 %all-gather.3.cloned.1.call-done = bf16[8,512,256]{2,1,0:T(8,128)(2,1)} async-done(((bf16[2,512,256]{2,1,0:T(8,128)(2,1)}), bf16[8,512,256]{2,1,0:T(8,128)(2,1)}) %all-gather.3.cloned.1.call-update) | async-done | bytes 2097168 | tf_op jit(solution)/shard_map/all_gather | solution.py:65
  359.7 2.8 reduce_sum.12
  362.5 1.7 fusion.5
  364.3 0.8 fusion.7
Async XLA Ops:
  7.2 95.2 %copy-start = (bf16[416,4096]{1,0:T(8,128)(2,1)S(1)}, bf16[416,4096]{1,0:T(8,128)(2,1)}, u32[]{:S(2)}) copy-start(bf16[416,4096]{1,0:T(8,128)(2,1)} %param.5) | copy-start | bytes 10223620
  7.2 95.2 %all-reduce.7.cloned.1.call-start = ((), (), s32[]{:S(2)}) async-start(), calls=%async_computation.6 | async-start | bytes 8388608 | tf_op jit(solution)/shard_map/psum | solution.py:10
  13.8 165.1 %reduce-scatter.5.cloned.1.call-start = ((), (), s32[]{:S(2)}) async-start(), calls=%async_computation.3 | async-start | bytes 2359296 | tf_op jit(solution)/shard_map/reduce_scatter | solution.py:60
  102.4 2.8 copy-start.3
  105.2 2.9 copy-start.11
  105.2 2.1 copy-start.1
  107.3 1.6 copy-start.9
  110.4 126.4 %all-reduce.5.cloned.1.call-start = ((), (), s32[]{:S(2)}) async-start(), calls=%async_computation.5 | async-start | bytes 4718592 | tf_op jit(solution)/shard_map/psum | solution.py:10
  179.0 156.2 %reduce-scatter.3.cloned.1.call-start = ((), (), s32[]{:S(2)}) async-start(), calls=%async_computation.2 | async-start | bytes 4718592 | tf_op jit(solution)/shard_map/reduce_scatter | solution.py:57
  236.8 3.6 copy-start.2
  236.8 3.6 copy-start.10
  236.8 3.8 %copy-start.13 = (bf16[128,4096]{1,0:T(8,128)(2,1)S(1)}, bf16[128,4096]{1,0:T(8,128)(2,1)}, u32[]{:S(2)}) copy-start(bf16[128,4096]{1,0:T(8,128)(2,1)} %get-tuple-element.4) | copy-start | bytes 3145732
  240.4 2.7 copy-start.7
  240.4 2.7 copy-start.8
  241.7 1.3 copy-start.5
  246.6 90.6 %copy-start.12 = (s32[2]{0:T(128)S(1)}, s32[2]{0:T(128)}, u32[]{:S(2)}) copy-start(s32[2]{0:T(128)} %param.9) | copy-start | bytes 28
  246.7 113.0 %all-gather.3.cloned.1.call-start = ((), (), s32[]{:S(2)}) async-start(), calls=%async_computation.4 | async-start | bytes 2621440 | tf_op jit(solution)/shard_map/all_gather | solution.py:65
  339.3 2.9 copy-start.4
  339.3 2.9 copy-start.6
Sparse Core Ops, SparseCore 0:
  14.0 88.3 all-reduce.6
  110.5 68.3 reduce-scatter.4
  181.7 55.1 all-reduce.4
  246.8 88.3 reduce-scatter.2
  337.3 22.3 all-gather.2
